TPU v7x, 32 devices: a whole 2x2x4 slice. The times are simulated.
32 devices in a mesh: dp: 8 (over y, x, core), fsdp: 4 (over z).
Axes of the slice: x: 2, y: 2, z: 4, core: 2. Of those that a mesh axis runs over, the one named last changes fastest.
Arguments:
- patches: bfloat16 [2, 2048, 1152], P(None, ('dp', 'fsdp')), may hold values from -6 to 6
- cotangent: bfloat16 [2, 2048, 1152], P(None, ('dp', 'fsdp')), may hold values from -6 to 6
- conditioning: float32 [2, 8, 1152], replicated, may hold values from -6 to 6
- frame_of_slot: int32 [2, 2048], P(None, ('dp', 'fsdp')), may hold values from 0 to 127, as said below
- clip_of_slot: int32 [2, 2048], P(None, ('dp', 'fsdp')), may hold values from 0 to 7, as said below
- w_ada: bfloat16 [1152, 6912], P('dp', 'fsdp'), may hold values from -0.1875 to 0.1875
- b_ada: bfloat16 [6912], P('fsdp'), may hold values from -3 to 3
- w_qkv: bfloat16 [1152, 3456], P('dp', 'fsdp'), may hold values from -0.1875 to 0.1875
- b_qv: bfloat16 [2304], P('fsdp'), may hold values from -2 to 2
- w_proj: bfloat16 [1152, 1152], P('dp', 'fsdp'), may hold values from -1 to 1
- b_proj: bfloat16 [1152], P('fsdp'), may hold values from -2 to 2
- w_fc1: bfloat16 [1152, 4608], P('dp', 'fsdp'), may hold values from -0.1875 to 0.1875
- b_fc1: bfloat16 [4608], P('fsdp'), may hold values from -3 to 3
- w_fc2: bfloat16 [4608, 1152], P('dp', 'fsdp'), may hold values from -0.09375 to 0.09375
- b_fc2: bfloat16 [1152], P('fsdp'), may hold values from -2 to 2
Outputs:
- output: bfloat16 [2, 2048, 1152], P(None, ('dp', 'fsdp'))
- input_grad: bfloat16 [2, 2048, 1152], P(None, ('dp', 'fsdp'))
- cond_grad: float32 [2, 8, 1152], P(None, None, 'fsdp')
- grad_w_ada: float32 [1152, 6912], P('dp', 'fsdp')
- grad_b_ada: float32 [6912], P('fsdp')
- grad_w_qkv: float32 [1152, 3456], P('dp', 'fsdp')
- grad_b_qv: float32 [2304], P('fsdp')
- grad_w_proj: float32 [1152, 1152], P('dp', 'fsdp')
- grad_b_proj: float32 [1152], P('fsdp')
- grad_w_fc1: float32 [1152, 4608], P('dp', 'fsdp')
- grad_b_fc1: float32 [4608], P('fsdp')
- grad_w_fc2: float32 [4608, 1152], P('dp', 'fsdp')
- grad_b_fc2: float32 [1152], P('fsdp')
Inputs may be any that keep to these rules, and one draw needn't show every extreme that they name: `frame_of_slot`: in each micro-batch, each aligned block of 64 slots holds either one frame of 64 patches or four frames of 16 patches one after another; no frame number appears in two blocks. `clip_of_slot`: all slots of one frame name the same clip.
All inputs are finite; a program needn't handle non-finite values.
Results may differ from a plain program's by a relative error of at most 0.018.
Values may be sent and summed in bfloat16 or wider, within the bound.
A program may use at most 256 MiB of HBM per device.

v0:
```python
import math
import jax
import jax.numpy as jnp
from jax import lax
from jax.sharding import PartitionSpec as P

HEAD_DIM = 72
EPS = 1e-06
GELU_C = math.sqrt(2.0 / math.pi)
PRECISE = lax.Precision.HIGHEST
NEG_FILL = -1e30


def layer_norm(values):
    centre = values - jnp.mean(values, axis=-1, keepdims=True)
    return centre * lax.rsqrt(jnp.mean(centre * centre, axis=-1, keepdims=True) + EPS)


def gelu_tanh(hidden):
    return 0.5 * hidden * (1.0 + jnp.tanh(GELU_C * (hidden + 0.044715 * hidden * hidden * hidden)))


def modulate(values, shift_part, scale_part):
    return layer_norm(values) * (1.0 + scale_part) + shift_part


def matmul_plain(left, right):
    return jnp.dot(left, right, preferred_element_type=jnp.float32)


def matmul_right_t(left, right):
    return lax.dot_general(
        left, right, (((1,), (1,)), ((), ())), preferred_element_type=jnp.float32
    )


def matmul_left_t(left, right):
    return lax.dot_general(
        left, right, (((0,), (0,)), ((), ())), preferred_element_type=jnp.float32
    )


def precise_left_t(left, right):
    return lax.dot_general(
        left, right, (((0,), (0,)), ((), ())), precision=PRECISE, preferred_element_type=jnp.float32
    )


def precise_right_t(left, right):
    return lax.dot_general(
        left, right, (((1,), (1,)), ((), ())), precision=PRECISE, preferred_element_type=jnp.float32
    )


def gather_weights(w_qkv, w_proj, w_fc1, w_fc2, b_qv, b_proj, b_fc1, b_fc2):
    inner_parts = (
        lax.all_gather(w_qkv, "fsdp", axis=1, tiled=True),
        lax.all_gather(w_proj, "fsdp", axis=1, tiled=True),
        lax.all_gather(w_fc1, "fsdp", axis=1, tiled=True),
        lax.all_gather(w_fc2, "fsdp", axis=1, tiled=True),
        lax.all_gather(b_qv, "fsdp", axis=0, tiled=True),
        lax.all_gather(b_proj, "fsdp", axis=0, tiled=True),
        lax.all_gather(b_fc1, "fsdp", axis=0, tiled=True),
        lax.all_gather(b_fc2, "fsdp", axis=0, tiled=True),
    )
    whole_rows = (
        lax.all_gather(inner_parts[0], "dp", axis=0, tiled=True),
        lax.all_gather(inner_parts[1], "dp", axis=0, tiled=True),
        lax.all_gather(inner_parts[2], "dp", axis=0, tiled=True),
        lax.all_gather(inner_parts[3], "dp", axis=0, tiled=True),
    )
    return (
        whole_rows[0],
        whole_rows[1],
        whole_rows[2],
        whole_rows[3],
        inner_parts[4],
        inner_parts[5],
        inner_parts[6],
        inner_parts[7],
    )


def reduce_grads(full_w, full_b):
    inner_sums = (
        lax.psum_scatter(
            full_w[0].astype(jnp.bfloat16), "fsdp", scatter_dimension=1, tiled=True
        ).astype(jnp.float32),
        lax.psum_scatter(
            full_w[1].astype(jnp.bfloat16), "fsdp", scatter_dimension=1, tiled=True
        ).astype(jnp.float32),
        lax.psum_scatter(
            full_w[2].astype(jnp.bfloat16), "fsdp", scatter_dimension=1, tiled=True
        ).astype(jnp.float32),
        lax.psum_scatter(
            full_w[3].astype(jnp.bfloat16), "fsdp", scatter_dimension=1, tiled=True
        ).astype(jnp.float32),
        lax.psum_scatter(
            full_b[0].astype(jnp.bfloat16), "fsdp", scatter_dimension=0, tiled=True
        ).astype(jnp.float32),
        lax.psum_scatter(
            full_b[1].astype(jnp.bfloat16), "fsdp", scatter_dimension=0, tiled=True
        ).astype(jnp.float32),
        lax.psum_scatter(
            full_b[2].astype(jnp.bfloat16), "fsdp", scatter_dimension=0, tiled=True
        ).astype(jnp.float32),
        lax.psum_scatter(
            full_b[3].astype(jnp.bfloat16), "fsdp", scatter_dimension=0, tiled=True
        ).astype(jnp.float32),
    )
    outer_sums = (
        lax.psum_scatter(
            inner_sums[0].astype(jnp.bfloat16), "dp", scatter_dimension=0, tiled=True
        ).astype(jnp.float32),
        lax.psum_scatter(
            inner_sums[1].astype(jnp.bfloat16), "dp", scatter_dimension=0, tiled=True
        ).astype(jnp.float32),
        lax.psum_scatter(
            inner_sums[2].astype(jnp.bfloat16), "dp", scatter_dimension=0, tiled=True
        ).astype(jnp.float32),
        lax.psum_scatter(
            inner_sums[3].astype(jnp.bfloat16), "dp", scatter_dimension=0, tiled=True
        ).astype(jnp.float32),
    )
    small_sums = lax.psum((inner_sums[4], inner_sums[5], inner_sums[6], inner_sums[7]), "dp")
    return (tuple(outer_sums), tuple(small_sums))


def modulation_sharded(silu_low, w_ada, b_ada):
    row_width, col_width = w_ada.shape
    row_start = lax.axis_index("dp") * row_width
    col_start = lax.axis_index("fsdp") * col_width
    silu_part = lax.dynamic_slice_in_dim(silu_low, row_start, row_width, 1)
    partial_value = matmul_plain(silu_part, w_ada)
    bias_term = jnp.where(
        lax.axis_index("dp") == 0, b_ada.astype(jnp.float32), jnp.zeros((col_width,), jnp.float32)
    )
    partial_value = partial_value + bias_term[None, :]
    padded = jnp.zeros((silu_low.shape[0], col_width * lax.axis_size("fsdp")), jnp.float32)
    padded = lax.dynamic_update_slice_in_dim(padded, partial_value, col_start, 1)
    return lax.psum(padded, ("dp", "fsdp"))


def ada_grads_sharded(silu_low, cond_rows, d_modulation, w_ada):
    row_width, col_width = w_ada.shape
    row_start = lax.axis_index("dp") * row_width
    col_start = lax.axis_index("fsdp") * col_width
    d_total = lax.psum(d_modulation, ("dp", "fsdp"))
    d_cols = lax.dynamic_slice_in_dim(d_total, col_start, col_width, 1)
    silu_part = lax.dynamic_slice_in_dim(silu_low, row_start, row_width, 1).astype(jnp.float32)
    grad_weight = precise_left_t(silu_part, d_cols)
    grad_bias = jnp.sum(d_cols, axis=0)
    d_silu_part = precise_right_t(d_cols, w_ada.astype(jnp.float32))
    model_width = cond_rows.shape[1]
    padded = jnp.zeros((cond_rows.shape[0], model_width), jnp.float32)
    padded = lax.dynamic_update_slice_in_dim(padded, d_silu_part, row_start, 1)
    d_silu = lax.psum(padded, ("dp", "fsdp"))
    own_width = model_width // lax.axis_size("fsdp")
    own_start = lax.axis_index("fsdp") * own_width
    d_silu_own = lax.dynamic_slice_in_dim(d_silu, own_start, own_width, 1)
    cond_own = lax.dynamic_slice_in_dim(cond_rows, own_start, own_width, 1)
    silu_own, silu_own_back = jax.vjp(jax.nn.silu, cond_own)
    cond_grad = silu_own_back(d_silu_own)[0]
    return (grad_weight, grad_bias, cond_grad)


def head_scores(queries, key_rows, same_frame):
    scores = jnp.einsum(
        "qhd,khd->hqk", queries, key_rows, preferred_element_type=jnp.float32
    ) * HEAD_DIM ** (-0.5)
    return jnp.where(same_frame[None, :, :], scores, NEG_FILL)


def micro_forward(patch_rows, modulation, frame_ids, clip_ids, weights):
    w_qkv, w_proj, w_fc1, w_fc2, b_qv, b_proj, b_fc1, b_fc2 = weights
    row_count, model_width = patch_rows.shape
    head_count = model_width // HEAD_DIM
    clip_hot = (
        clip_ids[:, None] == jnp.arange(modulation.shape[0], dtype=jnp.int32)[None, :]
    ).astype(jnp.float32)
    token_mod = jnp.dot(clip_hot, modulation, precision=PRECISE)
    shift_one, scale_one, gate_one, shift_two, scale_two, gate_two = jnp.split(token_mod, 6, axis=1)
    inputs_float = patch_rows.astype(jnp.float32)
    attn_in, norm_one_back = jax.vjp(modulate, inputs_float, shift_one, scale_one)
    attn_low = attn_in.astype(jnp.bfloat16)
    qkv_bias = jnp.concatenate(
        [b_qv[:model_width], jnp.zeros((model_width,), jnp.bfloat16), b_qv[model_width:]]
    ).astype(jnp.float32)
    qkv_low = (matmul_plain(attn_low, w_qkv) + qkv_bias).astype(jnp.bfloat16)
    queries = qkv_low[:, :model_width].reshape(row_count, head_count, HEAD_DIM)
    key_rows = qkv_low[:, model_width : 2 * model_width].reshape(row_count, head_count, HEAD_DIM)
    value_rows = qkv_low[:, 2 * model_width :].reshape(row_count, head_count, HEAD_DIM)
    same_frame = frame_ids[:, None] == frame_ids[None, :]
    scores = head_scores(queries, key_rows, same_frame)
    row_max = jnp.max(scores, axis=-1, keepdims=True)
    exp_scores = jnp.exp(scores - row_max)
    exp_total = jnp.sum(exp_scores, axis=-1, keepdims=True)
    shares = exp_scores / exp_total
    log_total = row_max + jnp.log(exp_total)
    mixed_low = (
        jnp.einsum(
            "hqk,khd->qhd",
            shares.astype(jnp.bfloat16),
            value_rows,
            preferred_element_type=jnp.float32,
        )
        .reshape(row_count, model_width)
        .astype(jnp.bfloat16)
    )
    attn_out = matmul_plain(mixed_low, w_proj) + b_proj.astype(jnp.float32)
    after_attn = inputs_float + gate_one * attn_out
    mlp_in, norm_two_back = jax.vjp(modulate, after_attn, shift_two, scale_two)
    mlp_low = mlp_in.astype(jnp.bfloat16)
    hidden = matmul_plain(mlp_low, w_fc1) + b_fc1.astype(jnp.float32)
    act_value, gelu_back = jax.vjp(gelu_tanh, hidden)
    act_low = act_value.astype(jnp.bfloat16)
    branch = matmul_plain(act_low, w_fc2) + b_fc2.astype(jnp.float32)
    output = (after_attn + gate_two * branch).astype(jnp.bfloat16)
    saved = (
        clip_hot,
        gate_one,
        gate_two,
        norm_one_back,
        attn_low,
        queries,
        key_rows,
        value_rows,
        same_frame,
        log_total,
        mixed_low,
        attn_out,
        norm_two_back,
        mlp_low,
        gelu_back,
        act_low,
        branch,
    )
    return (output, saved)


def micro_backward(saved, cot_rows, weights):
    w_qkv, w_proj, w_fc1, w_fc2 = (weights[0], weights[1], weights[2], weights[3])
    (
        clip_hot,
        gate_one,
        gate_two,
        norm_one_back,
        attn_low,
        queries,
        key_rows,
        value_rows,
        same_frame,
        log_total,
        mixed_low,
        attn_out,
        norm_two_back,
        mlp_low,
        gelu_back,
        act_low,
        branch,
    ) = saved
    row_count = cot_rows.shape[0]
    model_width = cot_rows.shape[1]
    head_count = model_width // HEAD_DIM
    cot_float = cot_rows.astype(jnp.float32)
    d_branch = (gate_two * cot_float).astype(jnp.bfloat16)
    grad_gate_two = cot_float * branch
    grad_w_fc2 = matmul_left_t(act_low, d_branch)
    grad_b_fc2 = jnp.sum(d_branch.astype(jnp.float32), axis=0)
    d_act = matmul_right_t(d_branch, w_fc2)
    d_hidden = gelu_back(d_act)[0].astype(jnp.bfloat16)
    grad_w_fc1 = matmul_left_t(mlp_low, d_hidden)
    grad_b_fc1 = jnp.sum(d_hidden.astype(jnp.float32), axis=0)
    d_mlp = matmul_right_t(d_hidden, w_fc1)
    d_after, d_shift_two, d_scale_two = norm_two_back(d_mlp)
    d_after = cot_float + d_after
    grad_gate_one = d_after * attn_out
    d_attn = (gate_one * d_after).astype(jnp.bfloat16)
    grad_w_proj = matmul_left_t(mixed_low, d_attn)
    grad_b_proj = jnp.sum(d_attn.astype(jnp.float32), axis=0)
    d_mix = (
        matmul_right_t(d_attn, w_proj).astype(jnp.bfloat16).reshape(row_count, head_count, HEAD_DIM)
    )
    shares_again = jnp.exp(head_scores(queries, key_rows, same_frame) - log_total)
    d_shares = jnp.einsum("qhd,khd->hqk", d_mix, value_rows, preferred_element_type=jnp.float32)
    row_delta = jnp.sum(shares_again * d_shares, axis=-1, keepdims=True)
    d_scores = (shares_again * (d_shares - row_delta)).astype(jnp.bfloat16)
    d_queries = jnp.einsum(
        "hqk,khd->qhd", d_scores, key_rows, preferred_element_type=jnp.float32
    ) * HEAD_DIM ** (-0.5)
    d_keys = jnp.einsum(
        "hqk,qhd->khd", d_scores, queries, preferred_element_type=jnp.float32
    ) * HEAD_DIM ** (-0.5)
    d_values = jnp.einsum(
        "hqk,qhd->khd", shares_again.astype(jnp.bfloat16), d_mix, preferred_element_type=jnp.float32
    )
    d_qkv = jnp.concatenate(
        [
            d_queries.reshape(row_count, model_width),
            d_keys.reshape(row_count, model_width),
            d_values.reshape(row_count, model_width),
        ],
        axis=1,
    ).astype(jnp.bfloat16)
    grad_w_qkv = matmul_left_t(attn_low, d_qkv)
    column_sums = jnp.sum(d_qkv.astype(jnp.float32), axis=0)
    grad_b_qv = jnp.concatenate([column_sums[:model_width], column_sums[2 * model_width :]])
    d_attn_in = matmul_right_t(d_qkv, w_qkv)
    d_inputs, d_shift_one, d_scale_one = norm_one_back(d_attn_in)
    input_grad = (d_after + d_inputs).astype(jnp.bfloat16)
    d_token_mod = jnp.concatenate(
        [d_shift_one, d_scale_one, grad_gate_one, d_shift_two, d_scale_two, grad_gate_two], axis=1
    )
    d_modulation = lax.dot_general(
        clip_hot,
        d_token_mod,
        (((0,), (0,)), ((), ())),
        precision=PRECISE,
        preferred_element_type=jnp.float32,
    )
    grads_w = (grad_w_qkv, grad_w_proj, grad_w_fc1, grad_w_fc2)
    grads_b = (grad_b_qv, grad_b_proj, grad_b_fc1, grad_b_fc2)
    return (input_grad, d_modulation, grads_w, grads_b)


def add_terms(first_terms, second_terms):
    if first_terms is None:
        return tuple(second_terms)
    return tuple(
        (first_item + second_item for first_item, second_item in zip(first_terms, second_terms))
    )


def per_device(
    patches,
    cotangent,
    conditioning,
    frame_of_slot,
    clip_of_slot,
    w_ada,
    b_ada,
    w_qkv,
    b_qv,
    w_proj,
    b_proj,
    w_fc1,
    b_fc1,
    w_fc2,
    b_fc2,
):
    micro_count = patches.shape[0]
    outputs = []
    input_grads = []
    cond_parts = []
    summed_w = None
    summed_b = None
    ada_terms = None
    for micro_index in range(micro_count):
        cond_rows = conditioning[micro_index]
        silu_value, silu_back = jax.vjp(jax.nn.silu, cond_rows)
        silu_low = silu_value.astype(jnp.bfloat16)
        weights = gather_weights(w_qkv, w_proj, w_fc1, w_fc2, b_qv, b_proj, b_fc1, b_fc2)
        modulation = modulation_sharded(silu_low, w_ada, b_ada)
        output, saved = micro_forward(
            patches[micro_index],
            modulation,
            frame_of_slot[micro_index],
            clip_of_slot[micro_index],
            weights,
        )
        input_grad, d_modulation, grads_w, grads_b = micro_backward(
            saved, cotangent[micro_index], weights
        )
        outputs.append(output)
        input_grads.append(input_grad)
        grad_w_ada, grad_b_ada, cond_grad = ada_grads_sharded(
            silu_low, cond_rows, d_modulation, w_ada
        )
        cond_parts.append(cond_grad[None])
        ada_terms = add_terms(ada_terms, (grad_w_ada, grad_b_ada))
        part_w, part_b = reduce_grads(grads_w, grads_b)
        summed_w = add_terms(summed_w, part_w)
        summed_b = add_terms(summed_b, part_b)
    cond_all = jnp.concatenate(cond_parts, axis=0)
    return (
        jnp.stack(outputs),
        jnp.stack(input_grads),
        cond_all,
        ada_terms[0],
        ada_terms[1],
        summed_w[0],
        summed_b[0],
        summed_w[1],
        summed_b[1],
        summed_w[2],
        summed_b[2],
        summed_w[3],
        summed_b[3],
    )


def solution(mesh):
    in_specs = (
        P(None, ("dp", "fsdp"), None),
        P(None, ("dp", "fsdp"), None),
        P(),
        P(None, ("dp", "fsdp")),
        P(None, ("dp", "fsdp")),
        P("dp", "fsdp"),
        P("fsdp"),
        P("dp", "fsdp"),
        P("fsdp"),
        P("dp", "fsdp"),
        P("fsdp"),
        P("dp", "fsdp"),
        P("fsdp"),
        P("dp", "fsdp"),
        P("fsdp"),
    )
    out_specs = (
        P(None, ("dp", "fsdp"), None),
        P(None, ("dp", "fsdp"), None),
        P(None, None, "fsdp"),
        P("dp", "fsdp"),
        P("fsdp"),
        P("dp", "fsdp"),
        P("fsdp"),
        P("dp", "fsdp"),
        P("fsdp"),
        P("dp", "fsdp"),
        P("fsdp"),
        P("dp", "fsdp"),
        P("fsdp"),
    )
    return jax.shard_map(
        per_device, mesh=mesh, in_specs=in_specs, out_specs=out_specs, check_vma=False
    )
```

profile of v0, /device:TPU:0, one launch (start us, length us, event | category | flops | bytes accessed | tf_op | source)
XLA Modules:
  0.0 1921.0 jit_solution(4469489425580298956)
XLA Ops:
  14.6 38.8 %all-gather = bf16[4,864,144]{1,2,0:T(8,128)(2,1)S(1)} all-gather(bf16[1,864,144]{1,2,0:T(8,128)(2,1)S(1)} %bitcast.245), channel_id=1, replica_groups=mesh['dp'=8,'fsdp'=4] {'fsdp'}, dimensions={0}, use_global_device_ids=true | all-gather | bytes 1244160 | tf_op jit(solution)/shard_map/all_gather | solution.py:57
  55.6 15.8 all-gather.1
  73.3 24.5 %all-gather.18.cloned.1.call-done = bf16[576,1152]{0,1:T(8,128)(2,1)} async-done(((bf16[576,288]{0,1:T(8,128)(2,1)}), bf16[576,1152]{0,1:T(8,128)(2,1)}) %all-gather.18.cloned.1.call-update) | async-done | bytes 1327120 | tf_op jit(solution)/shard_map/all_gather | solution.py:60
  102.9 16.8 all-reduce.16
  119.7 13.1 all-gather.2
  135.2 69.7 %all-reduce.25.cloned.1.call-done = (f32[8,6912]{1,0:T(8,128)}, f32[8,6912]{1,0:T(8,128)}) async-done(((f32[8,6912]{1,0:T(8,128)}, f32[8,6912]{1,0:T(8,128)}), (f32[8,6912]{1,0:T(8,128)}, f32[8,6912]{1,0:T(8,128)})) %all-reduce.25.cloned.1.call-update) | async-done | bytes 442384 | tf_op jit(solution)/shard_map/psum | solution.py:141
  217.8 6.2 fusion
  238.5 12.5 all-gather.16.cloned.1.call-done
  251.0 7.1 convolution_add_fusion.1
  258.2 58.6 %all-gather.20.cloned.1.call-done = bf16[4608,1152]{1,0:T(8,128)(2,1)} async-done(((bf16[576,1152]{1,0:T(8,128)(2,1)}), bf16[4608,1152]{1,0:T(8,128)(2,1)}) %all-gather.20.cloned.1.call-update) | async-done | bytes 10616848 | tf_op jit(solution)/shard_map/all_gather | solution.py:70
  316.8 8.8 fusion.139
  331.1 8.6 fusion.141
  363.6 6.0 fusion.160
  369.7 7.6 fusion.55
  378.1 20.2 %all-reduce.15 = (bf16[1152]{0:T(1024)(128)(2,1)S(1)}, bf16[2304]{0:T(1024)(128)(2,1)}, bf16[2304]{0:T(1024)(128)(2,1)}, bf16[1152]{0:T(1024)(128)(2,1)}, bf16[1...) all-reduce(bf16[1152]{0:T(1024)(128)(2,1)S(1)} %copy-done.101, ...), channel_id=1, replica_groups=mesh['dp'=8,'fsdp'=4] {'fsdp'}, use_global_device_ids=true, to_apply=%add.2 | all-reduce | flops 19584 | bytes 78336
  399.2 6.5 convolution_add_fusion.7
  437.4 5.6 convolution_convert_fusion
  456.2 14.8 copy.162
  477.7 15.3 copy.160
  493.1 315.4 %all-reduce.23.cloned.1.call-done = (f32[8,6912]{1,0:T(8,128)}, f32[8,6912]{1,0:T(8,128)}) async-done(((f32[8,6912]{1,0:T(8,128)}, f32[8,6912]{1,0:T(8,128)}), (f32[8,6912]{1,0:T(8,128)}, f32[8,6912]{1,0:T(8,128)})) %all-reduce.23.cloned.1.call-update) | async-done | bytes 442384 | tf_op jit(solution)/shard_map/psum | solution.py:148
  825.8 168.8 %reduce-scatter.47.cloned.1.call-done = bf16[4608,288]{0,1:T(8,128)(2,1)} async-done(((bf16[4608,1152]{0,1:T(8,128)(2,1)}), bf16[4608,288]{0,1:T(8,128)(2,1)}) %reduce-scatter.47.cloned.1.call-update) | async-done | bytes 2654224 | tf_op jit(solution)/shard_map/reduce_scatter | solution.py:95
  999.5 179.6 %reduce-scatter.45.cloned.1.call-done = bf16[4608,288]{0,1:T(8,128)(2,1)} async-done(((bf16[4608,1152]{0,1:T(8,128)(2,1)}), bf16[4608,288]{0,1:T(8,128)(2,1)}) %reduce-scatter.45.cloned.1.call-update) | async-done | bytes 2654224 | tf_op jit(solution)/shard_map/reduce_scatter | solution.py:95
  1183.8 179.3 %reduce-scatter.59.cloned.1.call-done = bf16[1152,1152]{1,0:T(8,128)(2,1)} async-done(((bf16[4608,1152]{1,0:T(8,128)(2,1)}), bf16[1152,1152]{1,0:T(8,128)(2,1)}) %reduce-scatter.59.cloned.1.call-update) | async-done | bytes 2654224
  1368.5 178.4 %reduce-scatter.57.cloned.1.call-done = bf16[1152,1152]{1,0:T(8,128)(2,1)} async-done(((bf16[4608,1152]{1,0:T(8,128)(2,1)}), bf16[1152,1152]{1,0:T(8,128)(2,1)}) %reduce-scatter.57.cloned.1.call-update) | async-done | bytes 2654224
  1557.3 24.7 %all-reduce.14 = (f32[576]{0:T(1024)}, f32[288]{0:T(512)}, f32[1152]{0:T(1024)}, f32[288]{0:T(512)}) all-reduce(f32[576]{0:T(1024)S(1)} %convert_add_fusion.7, f32[288]{0:T(512)S(1)} %convert_add_fusion.9, f32[1152]{0:T(1024)S(1)} %convert_add_fusion.6, f32[288]{0:T(512)S(1)} %convert_add_fusion.8), channel_id=1, replica_groups=mesh['dp'=8,'fsdp'=4] {'dp'}, use_global_device_ids=true, to_apply=%region_36.37 | all-reduce | flops 2304 | bytes 18432 | tf_op jit(solution)/shard_map/psum | solution.py:125
  1590.9 33.9 %reduce-scatter.53.cloned.1.call-done = bf16[144,288]{1,0:T(8,128)(2,1)} async-done(((bf16[1152,288]{1,0:T(8,128)(2,1)}), bf16[144,288]{1,0:T(8,128)(2,1)}) %reduce-scatter.53.cloned.1.call-update) | async-done | bytes 82960
  1626.6 42.2 %reduce-scatter.51.cloned.1.call-done = bf16[144,864]{1,0:T(8,128)(2,1)} async-done(((bf16[1152,864]{1,0:T(8,128)(2,1)}), bf16[144,864]{1,0:T(8,128)(2,1)}) %reduce-scatter.51.cloned.1.call-update) | async-done | bytes 248848
  1669.9 43.3 %reduce-scatter.49.cloned.1.call-done = bf16[144,864]{1,0:T(8,128)(2,1)} async-done(((bf16[1152,864]{1,0:T(8,128)(2,1)}), bf16[144,864]{1,0:T(8,128)(2,1)}) %reduce-scatter.49.cloned.1.call-update) | async-done | bytes 248848
  1715.6 49.3 %reduce-scatter.63.cloned.1.call-done = bf16[576,288]{1,0:T(8,128)(2,1)} async-done(((bf16[4608,288]{1,0:T(8,128)(2,1)}), bf16[576,288]{1,0:T(8,128)(2,1)}) %reduce-scatter.63.cloned.1.call-update) | async-done | bytes 331792
  1766.1 50.2 %reduce-scatter.61.cloned.1.call-done = bf16[576,288]{1,0:T(8,128)(2,1)} async-done(((bf16[4608,288]{1,0:T(8,128)(2,1)}), bf16[576,288]{1,0:T(8,128)(2,1)}) %reduce-scatter.61.cloned.1.call-update) | async-done | bytes 331792
  1818.5 45.1 %reduce-scatter.43.cloned.1.call-done = bf16[144,1152]{1,0:T(8,128)(2,1)} async-done(((bf16[1152,1152]{1,0:T(8,128)(2,1)}), bf16[144,1152]{1,0:T(8,128)(2,1)}) %reduce-scatter.43.cloned.1.call-update) | async-done | bytes 331792 | tf_op jit(solution)/shard_map/reduce_scatter | solution.py:118
  1863.5 47.7 %reduce-scatter.41.cloned.1.call-done = bf16[144,1152]{1,0:T(8,128)(2,1)} async-done(((bf16[1152,1152]{1,0:T(8,128)(2,1)}), bf16[144,1152]{1,0:T(8,128)(2,1)}) %reduce-scatter.41.cloned.1.call-update) | async-done | bytes 331792 | tf_op jit(solution)/shard_map/reduce_scatter | solution.py:118
  (539 shorter events, 184.6 us)
Async XLA Ops:
  8.0 64.7 %all-gather.14.cloned.1.call-start = ((), (), s32[]{:S(2)}) async-start(), calls=%async_computation.18 | async-start | bytes 1658880 | tf_op jit(solution)/shard_map/all_gather | solution.py:59
  8.8 89.0 %all-gather.18.cloned.1.call-start = ((), (), s32[]{:S(2)}) async-start(), calls=%async_computation.20 | async-start | bytes 1843200 | tf_op jit(solution)/shard_map/all_gather | solution.py:60
  9.5 195.4 %all-reduce.25.cloned.1.call-start = ((), (), s32[]{:S(2)}) async-start(), calls=%async_computation.40 | async-start | bytes 884736 | tf_op jit(solution)/shard_map/psum | solution.py:141
  14.6 195.0 %all-gather.10.cloned.1.call-start = ((), (), s32[]{:S(2)}) async-start(), calls=%async_computation.16 | async-start | bytes 8957952 | tf_op jit(solution)/shard_map/all_gather | solution.py:67
  55.6 172.4 %all-gather.12.cloned.1.call-start = ((), (), s32[]{:S(2)}) async-start(), calls=%async_computation.17 | async-start | bytes 2985984 | tf_op jit(solution)/shard_map/all_gather | solution.py:68
  72.6 178.4 %all-gather.16.cloned.1.call-start = ((), (), s32[]{:S(2)}) async-start(), calls=%async_computation.19 | async-start | bytes 11943936 | tf_op jit(solution)/shard_map/all_gather | solution.py:69
  73.3 60.7 %copy-start.17 = (bf16[2,64,1152]{2,1,0:T(8,128)(2,1)S(1)}, bf16[2,64,1152]{2,1,0:T(8,128)(2,1)}, u32[]{:S(2)}) copy-start(bf16[2,64,1152]{2,1,0:T(8,128)(2,1)} %param.15) | copy-start | bytes 884740
  73.3 243.5 %all-gather.20.cloned.1.call-start = ((), (), s32[]{:S(2)}) async-start(), calls=%async_computation.21 | async-start | bytes 11943936 | tf_op jit(solution)/shard_map/all_gather | solution.py:70
  100.4 708.0 %all-reduce.23.cloned.1.call-start = ((), (), s32[]{:S(2)}) async-start(), calls=%async_computation.39 | async-start | bytes 884736 | tf_op jit(solution)/shard_map/psum | solution.py:148
  134.1 75.1 %copy-start.106 = (f32[64]{0:T(128)}, f32[64]{0:T(128)S(1)}, u32[]{:S(2)}) copy-start(f32[64]{0:T(128)S(1)} %broadcast_multiply_fusion.3) | copy-start | bytes 772
  134.1 75.1 %copy-start.109 = (f32[64]{0:T(128)}, f32[64]{0:T(128)S(1)}, u32[]{:S(2)}) copy-start(f32[64]{0:T(128)S(1)} %broadcast_multiply_fusion.1) | copy-start | bytes 772
  134.9 74.3 %copy-start.129 = (f32[64]{0:T(128)}, f32[64]{0:T(128)S(1)}, u32[]{:S(2)}) copy-start(f32[64]{0:T(128)S(1)} %fusion.129) | copy-start | bytes 772
  135.0 74.3 %copy-start.131 = (f32[64]{0:T(128)}, f32[64]{0:T(128)S(1)}, u32[]{:S(2)}) copy-start(f32[64]{0:T(128)S(1)} %fusion.131) | copy-start | bytes 772
  135.0 72.7 %copy-start.118 = (s32[64]{0:T(128)}, s32[64]{0:T(128)S(1)}, u32[]{:S(2)}) copy-start(s32[64]{0:T(128)S(1)} %get-tuple-element.151) | copy-start | bytes 772
  135.0 72.7 %copy-start.120 = (s32[64]{0:T(128)}, s32[64]{0:T(128)S(1)}, u32[]{:S(2)}) copy-start(s32[64]{0:T(128)S(1)} %get-tuple-element.152) | copy-start | bytes 772
  417.3 395.2 %reduce-scatter.39.cloned.1.call-start = ((), (), s32[]{:S(2)}) async-start(), calls=%async_computation.25 | async-start | bytes 3317760 | tf_op jit(solution)/shard_map/reduce_scatter | solution.py:89
  420.1 394.8 %reduce-scatter.37.cloned.1.call-start = ((), (), s32[]{:S(2)}) async-start(), calls=%async_computation.24 | async-start | bytes 3317760 | tf_op jit(solution)/shard_map/reduce_scatter | solution.py:89
  423.5 393.9 %reduce-scatter.35.cloned.1.call-start = ((), (), s32[]{:S(2)}) async-start(), calls=%async_computation.23 | async-start | bytes 9953280 | tf_op jit(solution)/shard_map/reduce_scatter | solution.py:86
  430.1 391.6 %reduce-scatter.33.cloned.1.call-start = ((), (), s32[]{:S(2)}) async-start(), calls=%async_computation.22 | async-start | bytes 9953280 | tf_op jit(solution)/shard_map/reduce_scatter | solution.py:86
  436.5 558.1 %reduce-scatter.47.cloned.1.call-start = ((), (), s32[]{:S(2)}) async-start(), calls=%async_computation.29 | async-start | bytes 13271040 | tf_op jit(solution)/shard_map/reduce_scatter | solution.py:95
  443.1 735.9 %reduce-scatter.45.cloned.1.call-start = ((), (), s32[]{:S(2)}) async-start(), calls=%async_computation.28 | async-start | bytes 13271040 | tf_op jit(solution)/shard_map/reduce_scatter | solution.py:95
  449.6 913.6 %reduce-scatter.59.cloned.1.call-start = ((), (), s32[]{:S(2)}) async-start(), calls=%async_computation.35 | async-start | bytes 13271040
  471.0 1075.9 %reduce-scatter.57.cloned.1.call-start = ((), (), s32[]{:S(2)}) async-start(), calls=%async_computation.34 | async-start | bytes 13271040
  493.0 1094.6 %all-reduce.21.cloned.1.call-start = ((), (), s32[]{:S(2)}) async-start(), calls=%async_computation.38 | async-start | bytes 147456 | tf_op jit(solution)/shard_map/psum | solution.py:157
  812.5 777.4 %reduce-scatter.55.cloned.1.call-start = ((), (), s32[]{:S(2)}) async-start(), calls=%async_computation.33 | async-start | bytes 995328
  814.9 809.8 %reduce-scatter.53.cloned.1.call-start = ((), (), s32[]{:S(2)}) async-start(), calls=%async_computation.32 | async-start | bytes 995328
  817.4 851.4 %reduce-scatter.51.cloned.1.call-start = ((), (), s32[]{:S(2)}) async-start(), calls=%async_computation.31 | async-start | bytes 2322432
  821.6 891.6 %reduce-scatter.49.cloned.1.call-start = ((), (), s32[]{:S(2)}) async-start(), calls=%async_computation.30 | async-start | bytes 2322432
  825.8 939.0 %reduce-scatter.63.cloned.1.call-start = ((), (), s32[]{:S(2)}) async-start(), calls=%async_computation.37 | async-start | bytes 3981312
  999.4 816.9 %reduce-scatter.61.cloned.1.call-start = ((), (), s32[]{:S(2)}) async-start(), calls=%async_computation.36 | async-start | bytes 3981312
  1183.8 679.8 %reduce-scatter.43.cloned.1.call-start = ((), (), s32[]{:S(2)}) async-start(), calls=%async_computation.27 | async-start | bytes 2985984 | tf_op jit(solution)/shard_map/reduce_scatter | solution.py:118
  1368.4 542.8 %reduce-scatter.41.cloned.1.call-start = ((), (), s32[]{:S(2)}) async-start(), calls=%async_computation.26 | async-start | bytes 2985984 | tf_op jit(solution)/shard_map/reduce_scatter | solution.py:118
  (141 other events, 917.9 us)
Sparse Core Ops, SparseCore 0:
  10.5 50.6 all-gather.13
  62.9 34.8 all-gather.17
  100.4 51.8 all-gather.9
  154.8 30.4 all-gather.11
  187.2 63.8 all-gather.15
  252.9 63.8 all-gather.19
  420.4 50.7 reduce-scatter.38
  473.6 52.8 reduce-scatter.36
  528.8 138.6 reduce-scatter.34
  669.8 140.9 reduce-scatter.32
  813.2 181.4 reduce-scatter.46
  997.0 181.9 reduce-scatter.44
  1181.4 181.7 reduce-scatter.58
  1365.5 181.3 reduce-scatter.56
  1550.0 36.2 reduce-scatter.54
  1589.7 35.0 reduce-scatter.52
  1627.9 40.8 reduce-scatter.50
  1672.4 40.8 reduce-scatter.48
  1716.7 48.0 reduce-scatter.62
  1768.2 48.0 reduce-scatter.60
  1819.8 43.7 reduce-scatter.42
  1867.4 43.7 reduce-scatter.40
Sparse Core Ops, SparseCore 1:
  16.0 188.9 all-reduce.24
  417.4 391.0 all-reduce.22
  814.5 555.3 all-reduce.20
where the time goes:
time: 1930 us; the launch traced here: 1920 us
  waiting for transfers between devices  1500 us (78%)
  matrix products  134 us (7%)
  blocking collectives  129 us (7%)
  local copies, waits for them, and re-layouts  106 us (5%)
  other arithmetic  27.3 us (1%)
  between operations  21.9 us (1%)
    unnamed x33, waiting for transfers between devices  579 us
    reduce_scatter x2, waiting for transfers between devices, reduce_grads(): lax.psum_scatter(full_w[3].astype(jnp.bfloat16), 'fsdp', scatter_dimensio...  348 us
    psum x1, waiting for transfers between devices, ada_grads_sharded(): d_total = lax.psum(d_modulation, ('dp', 'fsdp'))  315 us
    reduce_scatter x2, waiting for transfers between devices, reduce_grads(): lax.psum_scatter(inner_sums[2].astype(jnp.bfloat16), 'dp', scatter_dimens...  92.7 us
    unnamed x328, local copies, waits for them, and re-layouts  89.1 us
    psum x1, waiting for transfers between devices, modulation_sharded(): return lax.psum(padded, ('dp', 'fsdp'))  69.7 us
    all_gather x1, waiting for transfers between devices, gather_weights(): lax.all_gather(inner_parts[3], 'dp', axis=0, tiled=True)  58.6 us
    dot_general x8, matrix products, matmul_right_t(): lax.dot_general(left, right, (((1,), (1,)), ((), ())), preferred_element_...  41 us
  transfers between devices with their start and end apart: 25, of which 16 were waited for; matrix products, arithmetic and copies ran while one was open for 9% of the time, Pallas kernels for 0%

commit v1 on v0

--- a/solution.py
+++ b/solution.py
@@ -138,7 +138,7 @@
     partial_value = partial_value + bias_term[None, :]
     padded = jnp.zeros((silu_low.shape[0], col_width * lax.axis_size("fsdp")), jnp.float32)
     padded = lax.dynamic_update_slice_in_dim(padded, partial_value, col_start, 1)
-    return lax.psum(padded, ("dp", "fsdp"))
+    return lax.psum(lax.psum(padded, "fsdp"), "dp")
 
 
 def ada_grads_sharded(silu_low, cond_rows, d_modulation, w_ada):

time: 1930 us -> 2270 us (1.18)
  waiting for transfers between devices: 1500 us -> 1850 us
    reduce_scatter x2, waiting for transfers between devices: 0.04 us -> 275 us  [reduce_grads(): lax.psum_scatter(full_w[0].astype(jnp.bfloat16), 'fsdp', scatter_dimensio...]
    psum x1, waiting for transfers between devices: 315 us -> 47.9 us  [ada_grads_sharded(): d_total = lax.psum(d_modulation, ('dp', 'fsdp'))]
    reduce_scatter x2, waiting for transfers between devices: 0.04 us -> 104 us  [reduce_grads(): lax.psum_scatter(full_w[1].astype(jnp.bfloat16), 'fsdp', scatter_dimensio...]
    psum x1, waiting for transfers between devices: 0.01 us -> 84.6 us  [ada_grads_sharded(): d_silu = lax.psum(padded, ('dp', 'fsdp'))]
    all_gather x1, waiting for transfers between devices: 0.02 us -> 49.9 us  [gather_weights(): lax.all_gather(inner_parts[0], 'dp', axis=0, tiled=True)]
    all_gather x1, waiting for transfers between devices: 12.5 us -> 55.8 us  [gather_weights(): lax.all_gather(inner_parts[2], 'dp', axis=0, tiled=True)]
    unnamed x33 -> x34, waiting for transfers between devices: 579 us -> 620 us
    psum x1 -> x2, waiting for transfers between devices: 69.7 us -> 58.6 us  [modulation_sharded(): return lax.psum(lax.psum(padded, 'fsdp'), 'dp')]
  transfers between devices with their start and end apart: 25 -> 26, of which waited for: 16 -> 25; matrix products, arithmetic and copies ran while one was open for 9% -> 8% of each run, Pallas kernels for 0% -> 0%
where the time goes in v1:
time: 2270 us; the launch traced here: 2260 us
  waiting for transfers between devices  1850 us (81%)
  matrix products  131 us (6%)
  blocking collectives  124 us (5%)
  local copies, waits for them, and re-layouts  106 us (5%)
  other arithmetic  26.8 us (1%)
    unnamed x34, waiting for transfers between devices  620 us
    reduce_scatter x2, waiting for transfers between devices, reduce_grads(): lax.psum_scatter(full_w[3].astype(jnp.bfloat16), 'fsdp', scatter_dimensio...  358 us
    reduce_scatter x2, waiting for transfers between devices, reduce_grads(): lax.psum_scatter(full_w[0].astype(jnp.bfloat16), 'fsdp', scatter_dimensio...  275 us
    reduce_scatter x2, waiting for transfers between devices, reduce_grads(): lax.psum_scatter(full_w[1].astype(jnp.bfloat16), 'fsdp', scatter_dimensio...  104 us
    reduce_scatter x2, waiting for transfers between devices, reduce_grads(): lax.psum_scatter(inner_sums[2].astype(jnp.bfloat16), 'dp', scatter_dimens...  92.6 us
    unnamed x302, local copies, waits for them, and re-layouts  88.2 us
    psum x1, waiting for transfers between devices, ada_grads_sharded(): d_silu = lax.psum(padded, ('dp', 'fsdp'))  84.6 us
    all_gather x1, waiting for transfers between devices, gather_weights(): lax.all_gather(inner_parts[3], 'dp', axis=0, tiled=True)  58.7 us
  transfers between devices with their start and end apart: 26, of which 25 were waited for; matrix products, arithmetic and copies ran while one was open for 8% of the time, Pallas kernels for 0%

profile of v1, /device:TPU:0, one launch (start us, length us, event | category | flops | bytes accessed | tf_op | source)
XLA Modules:
  0.0 2260.6 jit_solution(2335090400972777260)
XLA Ops:
  13.6 38.5 %all-reduce.29.cloned.1.call-done = (f32[8,6912]{1,0:T(8,128)}, f32[8,6912]{1,0:T(8,128)}) async-done(((f32[8,6912]{1,0:T(8,128)}, f32[8,6912]{1,0:T(8,128)}), (f32[8,6912]{1,0:T(8,128)}, f32[8,6912]{1,0:T(8,128)})) %all-reduce.29.cloned.1.call-update) | async-done | bytes 442384 | tf_op jit(solution)/shard_map/psum | solution.py:141
  52.2 29.3 %all-gather = bf16[4,864,144]{1,2,0:T(8,128)(2,1)S(1)} all-gather(bf16[1,864,144]{1,2,0:T(8,128)(2,1)S(1)} %bitcast.245), channel_id=1, replica_groups=mesh['dp'=8,'fsdp'=4] {'fsdp'}, dimensions={0}, use_global_device_ids=true | all-gather | bytes 1244160 | tf_op jit(solution)/shard_map/all_gather | solution.py:57
  83.7 19.8 all-gather.1
  105.6 31.0 %all-gather.18.cloned.1.call-done = bf16[576,1152]{0,1:T(8,128)(2,1)} async-done(((bf16[576,288]{0,1:T(8,128)(2,1)}), bf16[576,1152]{0,1:T(8,128)(2,1)}) %all-gather.18.cloned.1.call-update) | async-done | bytes 1327120 | tf_op jit(solution)/shard_map/all_gather | solution.py:60
  141.7 16.6 all-reduce.17
  173.3 20.0 all-reduce.27.cloned.1.call-done
  197.8 49.9 %all-gather.10.cloned.1.call-done = bf16[1152,3456]{1,0:T(8,128)(2,1)} async-done(((bf16[144,3456]{1,0:T(8,128)(2,1)}), bf16[1152,3456]{1,0:T(8,128)(2,1)}) %all-gather.10.cloned.1.call-update) | async-done | bytes 7962640 | tf_op jit(solution)/shard_map/all_gather | solution.py:67
  264.8 15.7 all-gather.12.cloned.1.call-done
  290.6 55.8 %all-gather.16.cloned.1.call-done = bf16[1152,4608]{1,0:T(8,128)(2,1)} async-done(((bf16[144,4608]{1,0:T(8,128)(2,1)}), bf16[1152,4608]{1,0:T(8,128)(2,1)}) %all-gather.16.cloned.1.call-update) | async-done | bytes 10616848 | tf_op jit(solution)/shard_map/all_gather | solution.py:69
  353.5 58.7 %all-gather.20.cloned.1.call-done = bf16[4608,1152]{1,0:T(8,128)(2,1)} async-done(((bf16[576,1152]{1,0:T(8,128)(2,1)}), bf16[4608,1152]{1,0:T(8,128)(2,1)}) %all-gather.20.cloned.1.call-update) | async-done | bytes 10616848 | tf_op jit(solution)/shard_map/all_gather | solution.py:70
  472.4 20.2 all-reduce.16
  550.2 15.2 copy.162
  572.0 15.3 copy.160
  587.4 47.9 %all-reduce.25.cloned.1.call-done = (f32[8,6912]{1,0:T(8,128)}, f32[8,6912]{1,0:T(8,128)}) async-done(((f32[8,6912]{1,0:T(8,128)}, f32[8,6912]{1,0:T(8,128)}), (f32[8,6912]{1,0:T(8,128)}, f32[8,6912]{1,0:T(8,128)})) %all-reduce.25.cloned.1.call-update) | async-done | bytes 442384 | tf_op jit(solution)/shard_map/psum | solution.py:148
  639.4 51.7 %reduce-scatter.39.cloned.1.call-done = bf16[1152,288]{0,1:T(8,128)(2,1)} async-done(((bf16[1152,1152]{0,1:T(8,128)(2,1)}), bf16[1152,288]{0,1:T(8,128)(2,1)}) %reduce-scatter.39.cloned.1.call-update) | async-done | bytes 663568 | tf_op jit(solution)/shard_map/reduce_scatter | solution.py:89
  693.5 52.3 %reduce-scatter.37.cloned.1.call-done = bf16[1152,288]{0,1:T(8,128)(2,1)} async-done(((bf16[1152,1152]{0,1:T(8,128)(2,1)}), bf16[1152,288]{0,1:T(8,128)(2,1)}) %reduce-scatter.37.cloned.1.call-update) | async-done | bytes 663568 | tf_op jit(solution)/shard_map/reduce_scatter | solution.py:89
  748.2 137.6 %reduce-scatter.35.cloned.1.call-done = bf16[1152,864]{0,1:T(8,128)(2,1)} async-done(((bf16[1152,3456]{0,1:T(8,128)(2,1)}), bf16[1152,864]{0,1:T(8,128)(2,1)}) %reduce-scatter.35.cloned.1.call-update) | async-done | bytes 1990672 | tf_op jit(solution)/shard_map/reduce_scatter | solution.py:86
  890.0 137.0 %reduce-scatter.33.cloned.1.call-done = bf16[1152,864]{0,1:T(8,128)(2,1)} async-done(((bf16[1152,3456]{0,1:T(8,128)(2,1)}), bf16[1152,864]{0,1:T(8,128)(2,1)}) %reduce-scatter.33.cloned.1.call-update) | async-done | bytes 1990672 | tf_op jit(solution)/shard_map/reduce_scatter | solution.py:86
  1031.1 178.8 %reduce-scatter.47.cloned.1.call-done = bf16[4608,288]{0,1:T(8,128)(2,1)} async-done(((bf16[4608,1152]{0,1:T(8,128)(2,1)}), bf16[4608,288]{0,1:T(8,128)(2,1)}) %reduce-scatter.47.cloned.1.call-update) | async-done | bytes 2654224 | tf_op jit(solution)/shard_map/reduce_scatter | solution.py:95
  1214.7 178.7 %reduce-scatter.45.cloned.1.call-done = bf16[4608,288]{0,1:T(8,128)(2,1)} async-done(((bf16[4608,1152]{0,1:T(8,128)(2,1)}), bf16[4608,288]{0,1:T(8,128)(2,1)}) %reduce-scatter.45.cloned.1.call-update) | async-done | bytes 2654224 | tf_op jit(solution)/shard_map/reduce_scatter | solution.py:95
  1398.2 178.6 %reduce-scatter.59.cloned.1.call-done = bf16[1152,1152]{1,0:T(8,128)(2,1)} async-done(((bf16[4608,1152]{1,0:T(8,128)(2,1)}), bf16[1152,1152]{1,0:T(8,128)(2,1)}) %reduce-scatter.59.cloned.1.call-update) | async-done | bytes 2654224
  1582.2 178.2 %reduce-scatter.57.cloned.1.call-done = bf16[1152,1152]{1,0:T(8,128)(2,1)} async-done(((bf16[4608,1152]{1,0:T(8,128)(2,1)}), bf16[1152,1152]{1,0:T(8,128)(2,1)}) %reduce-scatter.57.cloned.1.call-update) | async-done | bytes 2654224
  1770.8 24.6 %all-reduce.13 = (f32[576]{0:T(1024)}, f32[288]{0:T(512)}, f32[1152]{0:T(1024)}, f32[288]{0:T(512)}) all-reduce(f32[576]{0:T(1024)S(1)} %convert_add_fusion.7, f32[288]{0:T(512)S(1)} %convert_add_fusion.9, f32[1152]{0:T(1024)S(1)} %convert_add_fusion.6, f32[288]{0:T(512)S(1)} %convert_add_fusion.8), channel_id=1, replica_groups=mesh['dp'=8,'fsdp'=4] {'dp'}, use_global_device_ids=true, to_apply=%region_38.39 | all-reduce | flops 2304 | bytes 18432 | tf_op jit(solution)/shard_map/psum | solution.py:125
  1801.6 84.6 %all-reduce.23.cloned.1.call-done = (f32[8,1152]{1,0:T(8,128)}, f32[8,1152]{1,0:T(8,128)}) async-done(((f32[8,1152]{1,0:T(8,128)}, f32[8,1152]{1,0:T(8,128)}), (f32[8,1152]{1,0:T(8,128)}, f32[8,1152]{1,0:T(8,128)})) %all-reduce.23.cloned.1.call-update) | async-done | bytes 73744 | tf_op jit(solution)/shard_map/psum | solution.py:157
  1888.5 38.2 %reduce-scatter.55.cloned.1.call-done = bf16[144,288]{1,0:T(8,128)(2,1)} async-done(((bf16[1152,288]{1,0:T(8,128)(2,1)}), bf16[144,288]{1,0:T(8,128)(2,1)}) %reduce-scatter.55.cloned.1.call-update) | async-done | bytes 82960
  1927.7 37.5 %reduce-scatter.53.cloned.1.call-done = bf16[144,288]{1,0:T(8,128)(2,1)} async-done(((bf16[1152,288]{1,0:T(8,128)(2,1)}), bf16[144,288]{1,0:T(8,128)(2,1)}) %reduce-scatter.53.cloned.1.call-update) | async-done | bytes 82960
  1967.1 42.3 %reduce-scatter.51.cloned.1.call-done = bf16[144,864]{1,0:T(8,128)(2,1)} async-done(((bf16[1152,864]{1,0:T(8,128)(2,1)}), bf16[144,864]{1,0:T(8,128)(2,1)}) %reduce-scatter.51.cloned.1.call-update) | async-done | bytes 248848
  2010.6 43.5 %reduce-scatter.49.cloned.1.call-done = bf16[144,864]{1,0:T(8,128)(2,1)} async-done(((bf16[1152,864]{1,0:T(8,128)(2,1)}), bf16[144,864]{1,0:T(8,128)(2,1)}) %reduce-scatter.49.cloned.1.call-update) | async-done | bytes 248848
  2056.3 49.3 %reduce-scatter.63.cloned.1.call-done = bf16[576,288]{1,0:T(8,128)(2,1)} async-done(((bf16[4608,288]{1,0:T(8,128)(2,1)}), bf16[576,288]{1,0:T(8,128)(2,1)}) %reduce-scatter.63.cloned.1.call-update) | async-done | bytes 331792
  2106.9 50.2 %reduce-scatter.61.cloned.1.call-done = bf16[576,288]{1,0:T(8,128)(2,1)} async-done(((bf16[4608,288]{1,0:T(8,128)(2,1)}), bf16[576,288]{1,0:T(8,128)(2,1)}) %reduce-scatter.61.cloned.1.call-update) | async-done | bytes 331792
  2159.3 45.1 %reduce-scatter.43.cloned.1.call-done = bf16[144,1152]{1,0:T(8,128)(2,1)} async-done(((bf16[1152,1152]{1,0:T(8,128)(2,1)}), bf16[144,1152]{1,0:T(8,128)(2,1)}) %reduce-scatter.43.cloned.1.call-update) | async-done | bytes 331792 | tf_op jit(solution)/shard_map/reduce_scatter | solution.py:118
  2204.3 47.5 %reduce-scatter.41.cloned.1.call-done = bf16[144,1152]{1,0:T(8,128)(2,1)} async-done(((bf16[1152,1152]{1,0:T(8,128)(2,1)}), bf16[144,1152]{1,0:T(8,128)(2,1)}) %reduce-scatter.41.cloned.1.call-update) | async-done | bytes 331792 | tf_op jit(solution)/shard_map/reduce_scatter | solution.py:118
  (516 shorter events, 250.8 us)
Async XLA Ops:
  7.2 44.9 %all-reduce.29.cloned.1.call-start = ((), (), s32[]{:S(2)}) async-start(), calls=%async_computation.41 | async-start | bytes 884736 | tf_op jit(solution)/shard_map/psum | solution.py:141
  8.7 43.5 %copy-start.86 = (bf16[144,864]{1,0:T(8,128)(2,1)S(1)}, bf16[144,864]{1,0:T(8,128)(2,1)}, u32[]{:S(2)}) copy-start(bf16[144,864]{1,0:T(8,128)(2,1)} %param.22) | copy-start | bytes 746500
  12.0 92.8 %all-gather.14.cloned.1.call-start = ((), (), s32[]{:S(2)}) async-start(), calls=%async_computation.18 | async-start | bytes 1658880 | tf_op jit(solution)/shard_map/all_gather | solution.py:59
  12.8 123.8 %all-gather.18.cloned.1.call-start = ((), (), s32[]{:S(2)}) async-start(), calls=%async_computation.20 | async-start | bytes 1843200 | tf_op jit(solution)/shard_map/all_gather | solution.py:60
  13.5 179.8 %all-reduce.27.cloned.1.call-start = ((), (), s32[]{:S(2)}) async-start(), calls=%async_computation.40 | async-start | bytes 884736 | tf_op jit(solution)/shard_map/psum | solution.py:141
  52.1 195.6 %all-gather.10.cloned.1.call-start = ((), (), s32[]{:S(2)}) async-start(), calls=%async_computation.16 | async-start | bytes 8957952 | tf_op jit(solution)/shard_map/all_gather | solution.py:67
  83.7 196.8 %all-gather.12.cloned.1.call-start = ((), (), s32[]{:S(2)}) async-start(), calls=%async_computation.17 | async-start | bytes 2985984 | tf_op jit(solution)/shard_map/all_gather | solution.py:68
  104.8 241.6 %all-gather.16.cloned.1.call-start = ((), (), s32[]{:S(2)}) async-start(), calls=%async_computation.19 | async-start | bytes 11943936 | tf_op jit(solution)/shard_map/all_gather | solution.py:69
  105.5 52.8 %copy-start.109 = (bf16[1152]{0:T(1024)(128)(2,1)S(1)}, bf16[1152]{0:T(1024)(128)(2,1)}, u32[]{:S(2)}) copy-start(bf16[1152]{0:T(1024)(128)(2,1)} %param.27) | copy-start | bytes 6916
  105.6 66.0 %copy-start.121 = (bf16[288]{0:T(512)(128)(2,1)S(1)}, bf16[288]{0:T(512)(128)(2,1)}, u32[]{:S(2)}) copy-start(bf16[288]{0:T(512)(128)(2,1)} %param.29) | copy-start | bytes 1732
  105.6 66.5 %copy-start.17 = (bf16[2,64,1152]{2,1,0:T(8,128)(2,1)S(1)}, bf16[2,64,1152]{2,1,0:T(8,128)(2,1)}, u32[]{:S(2)}) copy-start(bf16[2,64,1152]{2,1,0:T(8,128)(2,1)} %param.15) | copy-start | bytes 884740
  105.6 306.7 %all-gather.20.cloned.1.call-start = ((), (), s32[]{:S(2)}) async-start(), calls=%async_computation.21 | async-start | bytes 11943936 | tf_op jit(solution)/shard_map/all_gather | solution.py:70
  139.3 496.0 %all-reduce.25.cloned.1.call-start = ((), (), s32[]{:S(2)}) async-start(), calls=%async_computation.39 | async-start | bytes 884736 | tf_op jit(solution)/shard_map/psum | solution.py:148
  197.8 54.6 %copy-start.41 = (bf16[64,1152]{1,0:T(8,128)(2,1)}, bf16[64,1152]{1,0:T(8,128)(2,1)S(1)}, u32[]{:S(2)}) copy-start(bf16[64,1152]{1,0:T(8,128)(2,1)S(1)} %get-tuple-element.142) | copy-start | bytes 442372
  197.8 58.0 %copy-start.39 = (bf16[64,1152]{1,0:T(8,128)(2,1)}, bf16[64,1152]{1,0:T(8,128)(2,1)S(1)}, u32[]{:S(2)}) copy-start(bf16[64,1152]{1,0:T(8,128)(2,1)S(1)} %get-tuple-element.141) | copy-start | bytes 442372
  511.5 179.6 %reduce-scatter.39.cloned.1.call-start = ((), (), s32[]{:S(2)}) async-start(), calls=%async_computation.25 | async-start | bytes 3317760 | tf_op jit(solution)/shard_map/reduce_scatter | solution.py:89
  514.4 231.4 %reduce-scatter.37.cloned.1.call-start = ((), (), s32[]{:S(2)}) async-start(), calls=%async_computation.24 | async-start | bytes 3317760 | tf_op jit(solution)/shard_map/reduce_scatter | solution.py:89
  517.7 368.1 %reduce-scatter.35.cloned.1.call-start = ((), (), s32[]{:S(2)}) async-start(), calls=%async_computation.23 | async-start | bytes 9953280 | tf_op jit(solution)/shard_map/reduce_scatter | solution.py:86
  524.2 502.8 %reduce-scatter.33.cloned.1.call-start = ((), (), s32[]{:S(2)}) async-start(), calls=%async_computation.22 | async-start | bytes 9953280 | tf_op jit(solution)/shard_map/reduce_scatter | solution.py:86
  530.6 679.4 %reduce-scatter.47.cloned.1.call-start = ((), (), s32[]{:S(2)}) async-start(), calls=%async_computation.29 | async-start | bytes 13271040 | tf_op jit(solution)/shard_map/reduce_scatter | solution.py:95
  537.1 856.4 %reduce-scatter.45.cloned.1.call-start = ((), (), s32[]{:S(2)}) async-start(), calls=%async_computation.28 | async-start | bytes 13271040 | tf_op jit(solution)/shard_map/reduce_scatter | solution.py:95
  543.6 1033.2 %reduce-scatter.59.cloned.1.call-start = ((), (), s32[]{:S(2)}) async-start(), calls=%async_computation.35 | async-start | bytes 13271040
  565.4 1195.0 %reduce-scatter.57.cloned.1.call-start = ((), (), s32[]{:S(2)}) async-start(), calls=%async_computation.34 | async-start | bytes 13271040
  587.3 1298.9 %all-reduce.23.cloned.1.call-start = ((), (), s32[]{:S(2)}) async-start(), calls=%async_computation.38 | async-start | bytes 147456 | tf_op jit(solution)/shard_map/psum | solution.py:157
  639.3 1287.4 %reduce-scatter.55.cloned.1.call-start = ((), (), s32[]{:S(2)}) async-start(), calls=%async_computation.33 | async-start | bytes 995328
  693.4 1271.8 %reduce-scatter.53.cloned.1.call-start = ((), (), s32[]{:S(2)}) async-start(), calls=%async_computation.32 | async-start | bytes 995328
  748.1 1261.3 %reduce-scatter.51.cloned.1.call-start = ((), (), s32[]{:S(2)}) async-start(), calls=%async_computation.31 | async-start | bytes 2322432
  889.9 1164.1 %reduce-scatter.49.cloned.1.call-start = ((), (), s32[]{:S(2)}) async-start(), calls=%async_computation.30 | async-start | bytes 2322432
  1031.1 1074.5 %reduce-scatter.63.cloned.1.call-start = ((), (), s32[]{:S(2)}) async-start(), calls=%async_computation.37 | async-start | bytes 3981312
  1214.7 942.4 %reduce-scatter.61.cloned.1.call-start = ((), (), s32[]{:S(2)}) async-start(), calls=%async_computation.36 | async-start | bytes 3981312
  1398.2 806.2 %reduce-scatter.43.cloned.1.call-start = ((), (), s32[]{:S(2)}) async-start(), calls=%async_computation.27 | async-start | bytes 2985984 | tf_op jit(solution)/shard_map/reduce_scatter | solution.py:118
  1582.1 669.8 %reduce-scatter.41.cloned.1.call-start = ((), (), s32[]{:S(2)}) async-start(), calls=%async_computation.26 | async-start | bytes 2985984 | tf_op jit(solution)/shard_map/reduce_scatter | solution.py:118
  (129 other events, 893.2 us)
Sparse Core Ops, SparseCore 0:
  12.2 39.9 all-reduce.28
  53.8 45.6 all-gather.13
  101.1 35.4 all-gather.17
  140.0 53.3 all-reduce.26
  195.8 51.8 all-gather.9
  250.2 30.2 all-gather.11
  282.5 63.8 all-gather.15
  348.4 63.8 all-gather.19
  511.6 123.6 all-reduce.24
  637.4 53.5 reduce-scatter.38
  693.4 52.3 reduce-scatter.36
  748.0 137.7 reduce-scatter.34
  888.3 138.6 reduce-scatter.32
  1029.2 180.6 reduce-scatter.46
  1212.3 181.1 reduce-scatter.44
  1395.7 181.1 reduce-scatter.58
  1579.2 181.1 reduce-scatter.56
  1766.5 119.6 all-reduce.22
  1889.5 37.1 reduce-scatter.54
  1930.1 35.0 reduce-scatter.52
  1968.6 40.7 reduce-scatter.50
  2013.2 40.8 reduce-scatter.48
  2057.5 48.0 reduce-scatter.62
  2109.0 48.0 reduce-scatter.60
  2160.6 43.7 reduce-scatter.42
  2208.1 43.7 reduce-scatter.40
